TPU v7x, 128 devices: a whole 4x4x4 slice. The times are simulated.
128 devices in a mesh: cfg: 2 (over y_hi), group: 16 (over y_lo, x, core), mp: 4 (over z).
Axes of the slice: x: 4, y: 4 (y_hi: 2, y_lo: 2; y = y_hi * 2 + y_lo), z: 4, core: 2. Of those that a mesh axis runs over, the one named last changes fastest.
Arguments:
- latents: float32 [16384, 64], P(('group', 'mp')), may hold values from -0.6 to 0.6
- text_hidden: bfloat16 [2, 8192, 3072], P('cfg', ('group', 'mp')), may hold values from -6 to 6
- w_img_in: bfloat16 [64, 3072], replicated, may hold values from -0.75 to 0.75
- w_img_qkv: bfloat16 [3072, 4608], P(None, 'mp'), may hold values from -1 to 1
- w_txt_kv: bfloat16 [3072, 3072], P(None, 'mp'), may hold values from -0.109375 to 0.109375
- q_gain: float32 [128], replicated, may hold values from 0.25 to 1.75
- k_gain: float32 [128], replicated, may hold values from 0.25 to 1.75
- w_out: bfloat16 [1536, 3072], replicated, may hold values from -1 to 1
- w_final: bfloat16 [3072, 64], replicated, may hold values from -0.109375 to 0.109375
- mod_img: float32 [8, 3, 3072], replicated, may hold values from -3 to 3
- mod_txt: float32 [8, 2, 3072], replicated, may hold values from -3 to 3
- mod_final: float32 [8, 2, 3072], replicated, may hold values from -3 to 3
- guide: float32 [16], replicated, may hold values from 1.5 to 5
- step_size: float32 [8], replicated, may hold values from 0.02 to 0.3
- img_len: int32 [16], replicated, may hold values from 1 to 1024, as said below
- txt_len: int32 [16], replicated, may hold values from 1 to 512, as said below
- split_flag: int32 [2, 16], replicated, may hold values from 0 to 1, as said below
- tstep: int32 [16], replicated, may hold values from 0 to 7
Outputs:
- velocity: float32 [2, 8192, 64], P('cfg', ('group', 'mp'))
- next_latents: float32 [2, 8192, 64], P('cfg', ('group', 'mp'))
Inputs may be any that keep to these rules, and one draw needn't show every extreme that they name: `img_len`: some group has exactly 1024 live image tokens. `txt_len`: some group has exactly 512 live text tokens. `split_flag`: entries [c, 2j] and [c, 2j + 1] are equal; at least one such pair carries 1 and at least one carries 0.
All inputs are finite; a program needn't handle non-finite values.
Results may differ from a plain program's by a relative error of at most 0.035.
Values may be sent and summed in bfloat16 or wider, within the bound.
A program may use at most 192 MiB of HBM per device.

v0:
```python
import jax
import jax.numpy as jnp
from jax import lax
from jax.sharding import PartitionSpec as P

HD = 128


def partner(value, axis, bit):
    mask = 2**bit
    pairs = [(source, source ^ mask) for source in range(lax.axis_size(axis))]
    return lax.ppermute(value, axis, pairs)


def layer_norm(values):
    center = values - jnp.mean(values, -1, keepdims=True)
    spread = jnp.mean(center * center, -1, keepdims=True)
    return center * lax.rsqrt(spread + 1e-06)


def head_norm(values, gain):
    return values * lax.rsqrt(jnp.mean(values * values, -1, keepdims=True) + 1e-06) * gain


def pick_entry(table, index):
    return lax.dynamic_index_in_dim(table, index, 0, keepdims=False)


def local(
    latents,
    text_hidden,
    w_img_in,
    w_img_qkv,
    w_txt_kv,
    q_gain,
    k_gain,
    w_out,
    w_final,
    mod_img,
    mod_txt,
    mod_final,
    guide,
    step_size,
    img_len,
    txt_len,
    split_flag,
    tstep,
):
    group_index = lax.axis_index("group")
    mp_index = lax.axis_index("mp")
    cfg_index = lax.axis_index("cfg")
    mp_count = lax.axis_size("mp")
    mate_index = jnp.bitwise_xor(group_index, 1)
    step_index = pick_entry(tstep, group_index)
    mod_rows = pick_entry(mod_img, step_index)
    text_rows = pick_entry(mod_txt, step_index)
    final_rows = pick_entry(mod_final, step_index)
    shard_rows = latents.shape[0]
    half_rows = shard_rows // 2
    full_img = shard_rows * mp_count
    full_txt = text_hidden.shape[1] * mp_count
    local_heads = w_img_qkv.shape[1] // (3 * HD)
    x_img = jnp.dot(latents.astype(jnp.bfloat16), w_img_in, preferred_element_type=jnp.float32)
    img_mod = (layer_norm(x_img) * (1.0 + mod_rows[1]) + mod_rows[0]).astype(jnp.bfloat16)
    txt_mod = (
        layer_norm(text_hidden[0].astype(jnp.float32)) * (1.0 + text_rows[1]) + text_rows[0]
    ).astype(jnp.bfloat16)
    img_full, txt_full = (
        lax.all_gather(img_mod, "mp", axis=0, tiled=True),
        lax.all_gather(txt_mod, "mp", axis=0, tiled=True),
    )
    qkv = jnp.dot(img_full, w_img_qkv, preferred_element_type=jnp.float32).reshape(
        full_img, local_heads, 3, HD
    )
    query = head_norm(qkv[:, :, 0], q_gain).astype(jnp.bfloat16)
    key_img = head_norm(qkv[:, :, 1], k_gain).astype(jnp.bfloat16)
    value_img = qkv[:, :, 2].astype(jnp.bfloat16)
    text_kv = jnp.dot(txt_full, w_txt_kv, preferred_element_type=jnp.float32).reshape(
        full_txt, local_heads, 2, HD
    )
    key_txt = head_norm(text_kv[:, :, 0], k_gain).astype(jnp.bfloat16)
    value_txt = text_kv[:, :, 1].astype(jnp.bfloat16)
    key_rows = jnp.concatenate([key_txt, key_img], axis=0)
    value_rows = jnp.concatenate([value_txt, value_img], axis=0)
    mate_keys, mate_values = partner((key_rows, value_rows), "group", 0)
    spots_txt = jnp.arange(full_txt, dtype=jnp.int32)
    spots_img = jnp.arange(full_img, dtype=jnp.int32)

    def live_rows(index):
        return jnp.concatenate(
            [spots_txt < pick_entry(txt_len, index), spots_img < pick_entry(img_len, index)]
        )

    flagged = pick_entry(pick_entry(split_flag, cfg_index), group_index) == 1
    live = jnp.concatenate([live_rows(group_index), live_rows(mate_index) & flagged])
    all_keys = jnp.concatenate([key_rows, mate_keys], axis=0)
    all_values = jnp.concatenate([value_rows, mate_values], axis=0)
    scores = jnp.einsum(
        "qhe,khe->hqk", query, all_keys, preferred_element_type=jnp.float32
    ) * HD ** (-0.5)
    scores = jnp.where(live[None, None, :], scores, -1e30)
    weights = jnp.exp(scores - jnp.max(scores, -1, keepdims=True))
    probs = (weights / jnp.sum(weights, -1, keepdims=True)).astype(jnp.bfloat16)
    mixed = jnp.einsum(
        "hqk,khe->qhe", probs, all_values, preferred_element_type=jnp.float32
    ).astype(jnp.bfloat16)
    mixed = mixed.reshape(full_img, local_heads * HD)
    w_local = lax.dynamic_slice_in_dim(w_out, mp_index * local_heads * HD, local_heads * HD, 0)
    attended = lax.psum_scatter(
        jnp.dot(mixed, w_local, preferred_element_type=jnp.float32),
        "mp",
        scatter_dimension=0,
        tiled=True,
    )
    hidden = x_img + mod_rows[2] * attended
    final = (layer_norm(hidden) * (1.0 + final_rows[1]) + final_rows[0]).astype(jnp.bfloat16)
    own_velocity = jnp.dot(final, w_final, preferred_element_type=jnp.float32)
    scale = pick_entry(guide, group_index)
    other_velocity = partner(own_velocity.astype(jnp.bfloat16), "cfg", 0).astype(own_velocity.dtype)
    is_cond = cfg_index == 0
    cond_part = jnp.where(is_cond, own_velocity, other_velocity)
    uncond_part = jnp.where(is_cond, other_velocity, own_velocity)
    guided_all = uncond_part + scale * (cond_part - uncond_part)
    guided = lax.dynamic_slice_in_dim(guided_all, cfg_index * half_rows, half_rows, 0)
    row_place = (
        mp_index * shard_rows + cfg_index * half_rows + jnp.arange(half_rows, dtype=jnp.int32)
    )
    row_live = row_place < pick_entry(img_len, group_index)
    guided = jnp.where(row_live[:, None], guided, 0.0)
    start_rows = lax.dynamic_slice_in_dim(latents, cfg_index * half_rows, half_rows, 0)
    moved = start_rows - pick_entry(step_size, step_index) * guided
    return (guided[None], moved[None])


def solution(mesh):
    placed = (
        P(("group", "mp"), None),
        P("cfg", ("group", "mp"), None),
        P(),
        P(None, "mp"),
        P(None, "mp"),
        P(),
        P(),
        P(),
        P(),
        P(),
        P(),
        P(),
        P(),
        P(),
        P(),
        P(),
        P(),
        P(),
    )
    return jax.shard_map(
        local,
        mesh=mesh,
        in_specs=placed,
        out_specs=(P("cfg", ("group", "mp"), None), P("cfg", ("group", "mp"), None)),
        check_vma=False,
    )
```

profile of v0, /device:TPU:1, one launch (start us, length us, event | category | flops | bytes accessed | tf_op | source)
XLA Modules:
  0.0 342.4 jit_solution(17559711383967402021)
XLA Ops:
  7.2 1.3 dynamic_slice.51
  9.8 1.3 convert_reduce_fusion
  11.1 1.5 fusion.18
  14.3 2.4 fusion.21
  16.8 1.5 fusion.50
  18.8 1.6 constant_dynamic-slice_fusion
  20.3 1.8 add_convert_fusion.1
  25.1 34.8 %all-gather.3.cloned.1.call-done = bf16[512,3072]{1,0:T(8,128)(2,1)} async-done(((bf16[128,3072]{1,0:T(8,128)(2,1)}), bf16[512,3072]{1,0:T(8,128)(2,1)}) %all-gather.3.cloned.1.call-update) | async-done | bytes 3145744 | tf_op jit(solution)/shard_map/all_gather | solution.py:70
  59.9 7.0 %fusion.53 = f32[512,768]{1,0:T(8,128)} fusion(bf16[512,3072]{1,0:T(8,128)(2,1)} %all-gather.3.cloned.1.call-done, bf16[3072,768]{1,0:T(8,128)(2,1)} %param.22), kind=kOutput, calls=%fused_computation.97 | convolution fusion | flops 2415919104 | bytes 9437184 | tf_op jit(solution)/shard_map/dot_general | solution.py:78
  66.9 2.9 reshape.125
  69.8 2.1 slice.60
  72.5 55.0 %all-gather.5.cloned.1.call-done = bf16[1024,3072]{1,0:T(8,128)(2,1)} async-done(((bf16[256,3072]{1,0:T(8,128)(2,1)}), bf16[1024,3072]{1,0:T(8,128)(2,1)}) %all-gather.5.cloned.1.call-update) | async-done | bytes 6291472 | tf_op jit(solution)/shard_map/all_gather | solution.py:69
  127.5 11.3 %fusion.54 = f32[1024,1152]{0,1:T(8,128)S(1)} fusion(bf16[1024,3072]{1,0:T(8,128)(2,1)} %all-gather.5.cloned.1.call-done, bf16[3072,1152]{1,0:T(8,128)(2,1)} %param.21), kind=kOutput, calls=%fused_computation.98 | convolution fusion | flops 7247757312 | bytes 18087936 | tf_op jit(solution)/shard_map/dot_general | solution.py:72
  138.8 2.1 copy-done.2
  140.9 1.3 slice.61
  142.2 3.0 copy.40
  145.2 1.9 fusion.22
  147.1 1.9 fusion.24
  152.4 1.3 dynamic_slice.57
  154.9 3.1 slice.57
  158.0 2.9 copy.41
  160.9 1.5 fusion.30
  163.3 2.1 pad_maximum_fusion.1
  165.4 1.6 multiply_reduce_fusion.2
  167.0 19.6 %fusion.51 = (f32[3,1024]{1,0:T(4,128)}, f32[3,1024,3072]{2,1,0:T(8,128)}) fusion(pred[3072]{0:T(1024)(128)(4,1)} %pad_add_fusion, bf16[1536,3,128]{2,0,1:T(8,128)(2,1)} %collective-permute-done.1, bf16[1024,3,128]{2,0,1:T(8,128)(2,1)} %copy-done.4, bf16[512,3,128]{2,0,1:T(8,128)(2,1)S(1)} %multiply_convert_fusion.1, f32[1024,3,3,128]{0,3,2,1:T(8,128)} %bitcast.91, ...), kind=kOutput, calls=%fused_computation.95 | convolution fusion | flops 2461928448 | bytes 41709056 | tf_op jit(solution)/shard_map/sub | solution.py:102
  186.6 15.0 %fusion.26 = bf16[3,128,1024]{2,1,0:T(8,128)(2,1)S(1)} fusion(f32[3,1024,3072]{2,1,0:T(8,128)} %get-tuple-element.19, f32[3,1024]{1,0:T(4,128)} %get-tuple-element.18, bf16[1536,3,128]{0,2,1:T(8,128)(2,1)} %collective-permute-done, bf16[1024,3,128]{0,2,1:T(8,128)(2,1)} %copy-done.3, bf16[512,3,128]{0,2,1:T(8,128)(2,1)} %bitcast.93), kind=kOutput, calls=%fused_computation.42 | convolution fusion | flops 2442264576 | bytes 40906752 | tf_op jit(solution)/shard_map/hqk,khe->qhe/dot_general | solution.py:104
  201.7 8.1 %fusion.13 = f32[1024,3072]{1,0:T(8,128)} fusion(bf16[1024,384]{0,1:T(8,128)(2,1)S(1)} %bitcast.94, bf16[1536,3072]{1,0:T(8,128)(2,1)} %param.25, s32[]{:T(128)S(6)} %select_n.66), kind=kOutput, calls=%fused_computation.21 | convolution fusion | flops 2415919104 | bytes 15728644 | tf_op jit(solution)/shard_map/dot_general | solution.py:110
  209.8 1.4 dynamic-slice_add_fusion
  211.2 113.8 %reduce-scatter.2.cloned.1.call-done = f32[256,3072]{1,0:T(8,128)} async-done(((f32[1024,3072]{1,0:T(8,128)}), f32[256,3072]{1,0:T(8,128)}) %reduce-scatter.2.cloned.1.call-update) | async-done | bytes 3145744 | tf_op jit(solution)/shard_map/reduce_scatter | solution.py:109
  325.0 2.3 fusion.47
  329.2 2.8 collective-permute-start.2
  334.0 1.9 subtract_bitcast_fusion
  (64 shorter events, 13.6 us)
Async XLA Ops:
  7.2 9.6 %copy-start = (bf16[64,3072]{1,0:T(8,128)(2,1)S(1)}, bf16[64,3072]{1,0:T(8,128)(2,1)}, u32[]{:S(2)}) copy-start(bf16[64,3072]{1,0:T(8,128)(2,1)} %param.20) | copy-start | bytes 1179652
  7.2 52.7 %all-gather.3.cloned.1.call-start = ((), (), s32[]{:S(2)}) async-start(), calls=%async_computation.1 | async-start | bytes 3932160 | tf_op jit(solution)/shard_map/all_gather | solution.py:70
  16.7 110.7 %all-gather.5.cloned.1.call-start = ((), (), s32[]{:S(2)}) async-start(), calls=%async_computation.2 | async-start | bytes 7864320 | tf_op jit(solution)/shard_map/all_gather | solution.py:69
  20.3 2.1 copy-start.8
  20.3 2.1 copy-start.9
  22.2 302.8 %reduce-scatter.2.cloned.1.call-start = ((), (), s32[]{:S(2)}) async-start(), calls=%async_computation.3 | async-start | bytes 15728640 | tf_op jit(solution)/shard_map/reduce_scatter | solution.py:109
  66.9 5.3 %copy-start.10 = (f32[128]{0:T(128)S(1)}, f32[128]{0:T(128)}, u32[]{:S(2)}) copy-start(f32[128]{0:T(128)} %param.24) | copy-start | bytes 1540
  138.8 2.2 copy-start.2
  149.0 0.9 copy-start.4
  151.0 16.0 %collective-permute-start.1 = (bf16[1536,3,128]{2,0,1:T(8,128)(2,1)}, bf16[1536,3,128]{2,0,1:T(8,128)(2,1)}, u32[]{:S(2)}, u32[]{:S(2)}) collective-permute-start(bf16[1536,3,128]{2,0,1:T(8,128)(2,1)} %pad_maximum_fusion.2), channel_id=1, source_target_pairs={{0,4},{4,0},{8,12},{12,8},{16,20},{20,16},{24,28},{28,24},{32,36},... | collective-permute-start | bytes 3538952 | tf_op jit(solution)/shard_map/ppermute | solution.py:12
  162.4 0.9 copy-start.3
  165.4 21.2 %collective-permute-start = (bf16[1536,3,128]{0,2,1:T(8,128)(2,1)}, bf16[1536,3,128]{0,2,1:T(8,128)(2,1)}, u32[]{:S(2)}, u32[]{:S(2)}) collective-permute-start(bf16[1536,3,128]{0,2,1:T(8,128)(2,1)} %pad_maximum_fusion.1), channel_id=1, source_target_pairs={{0,4},{4,0},{8,12},{12,8},{16,20},{20,16},{24,28},{28,24},{32,36},... | collective-permute-start | bytes 3538952 | tf_op jit(solution)/shard_map/ppermute | solution.py:12
  209.8 115.3 %copy-start.6 = (f32[1,1,3072]{2,0,1:T(1,128)S(1)}, f32[1,1,3072]{2,0,1:T(1,128)}, u32[]{:S(2)}) copy-start(f32[1,1,3072]{2,0,1:T(1,128)} %get-tuple-element.4) | copy-start | bytes 36868
  327.4 0.7 copy-start.7
  327.4 1.1 copy-start.11
  327.4 8.5 %copy-start.1 = (bf16[64,3072]{1,0:T(8,128)(2,1)S(1)}, bf16[64,3072]{1,0:T(8,128)(2,1)}, u32[]{:S(2)}) copy-start(bf16[64,3072]{1,0:T(8,128)(2,1)} %param.20) | copy-start | bytes 1179652
  327.4 5.3 %copy-start.12 = (f32[8]{0:T(128)S(1)}, f32[8]{0:T(128)}, u32[]{:S(2)}) copy-start(f32[8]{0:T(128)} %param.31) | copy-start | bytes 100
  327.4 6.0 %copy-start.13 = (f32[16]{0:T(128)S(1)}, f32[16]{0:T(128)}, u32[]{:S(2)}) copy-start(f32[16]{0:T(128)} %param.30) | copy-start | bytes 196
  327.4 6.6 %copy-start.5 = (f32[256,64]{0,1:T(8,128)S(1)}, f32[256,64]{0,1:T(8,128)}, u32[]{:S(2)}) copy-start(f32[256,64]{0,1:T(8,128)} %param.18) | copy-start | bytes 196612
  329.2 4.8 %collective-permute-start.2 = (bf16[256,64]{0,1:T(8,128)(2,1)S(1)}, bf16[256,64]{0,1:T(8,128)(2,1)S(1)}, u32[]{:S(2)}, u32[]{:S(2)}) collective-permute-start(bf16[256,64]{0,1:T(8,128)(2,1)S(1)} %get-tuple-element.20), channel_id=1, source_target_pairs={{0,64},{64,0},{1,65},{65,1},{2,66},{66,2},{3,67},{67,3},{4,68},{68... | collective-permute-start | bytes 98312 | tf_op jit(solution)/shard_map/ppermute | solution.py:12
Sparse Core Ops, SparseCore 0:
  16.8 42.9 all-gather.2
  61.5 65.8 all-gather.4
  209.9 115.0 reduce-scatter.1
where the time goes:
time: 343 us; the launch traced here: 342 us
  waiting for transfers between devices  204 us (59%)
  matrix products  63.3 us (18%)
  other arithmetic  27.7 us (8%)
  local copies, waits for them, and re-layouts  27.4 us (8%)
  between operations  16.7 us (5%)
  starting transfers between devices  3.83 us (1%)
    reduce_scatter x1, waiting for transfers between devices, local(): lax.psum_scatter(jnp.dot(mixed, w_local, preferred_element_type=jnp.float...  114 us
    all_gather x1, waiting for transfers between devices, local(): lax.all_gather(img_mod, 'mp', axis=0, tiled=True)  55 us
    all_gather x1, waiting for transfers between devices, local(): lax.all_gather(txt_mod, 'mp', axis=0, tiled=True)  34.8 us
    sub x1, matrix products, local(): weights = jnp.exp(scores - jnp.max(scores, -1, keepdims=True))  19.6 us
    dot_general x1, matrix products, local(): jnp.einsum('hqk,khe->qhe', probs, all_values, preferred_element_type=jnp....  15 us
    dot_general x1, matrix products, local(): jnp.dot(img_full, w_img_qkv, preferred_element_type=jnp.float32)  11.3 us
    unnamed x30, local copies, waits for them, and re-layouts  10.4 us
    dot_general x1, matrix products, local(): jnp.dot(mixed, w_local, preferred_element_type=jnp.float32)  8.09 us
  transfers between devices with their start and end apart: 6, of which 3 were waited for; matrix products, arithmetic and copies ran while one was open for 17% of the time, Pallas kernels for 0%

commit v1 on v0

--- a/solution.py
+++ b/solution.py
@@ -67,7 +67,9 @@
     ).astype(jnp.bfloat16)
     img_full, txt_full = (
         lax.all_gather(img_mod, "mp", axis=0, tiled=True),
-        lax.all_gather(txt_mod, "mp", axis=0, tiled=True),
+        jnp.concatenate(
+            lax.all_to_all(jnp.stack([txt_mod] * lax.axis_size("mp")), "mp", 0, 0), axis=0
+        ),
     )
     qkv = jnp.dot(img_full, w_img_qkv, preferred_element_type=jnp.float32).reshape(
         full_img, local_heads, 3, HD

time: 343 us -> 329 us (0.959)
  waiting for transfers between devices: 204 us -> 183 us
  starting transfers between devices: 3.83 us -> 9.21 us
    all_to_all x0 -> x1, waiting for transfers between devices: none -> 56.4 us  [local(): lax.all_to_all(jnp.stack([txt_mod] * lax.axis_size('mp')), 'mp', 0, 0)]
    all_gather x1, waiting for transfers between devices: 55 us -> 13.7 us  [local(): lax.all_gather(img_mod, 'mp', axis=0, tiled=True)]
    all_gather x1 -> x0, waiting for transfers between devices: 34.8 us -> none  [local(): lax.all_gather(txt_mod, 'mp', axis=0, tiled=True)]
    dot_general x0 -> x1, local copies, waits for them, and re-layouts: none -> 7 us  [local(): jnp.dot(txt_full, w_txt_kv, preferred_element_type=jnp.float32)]
    all_to_all x0 -> x1, starting transfers between devices: none -> 5.85 us  [local(): lax.all_to_all(jnp.stack([txt_mod] * lax.axis_size('mp')), 'mp', 0, 0)]
    slice x2 -> x0, local copies, waits for them, and re-layouts: 5.24 us -> none  [the longest x1 3.13 us: local(): value_txt = text_kv[:, :, 1].astype(jnp.bfloat16)]
    convert_element_type x0 -> x2, local copies, waits for them, and re-layouts: none -> 3.87 us  [local(): value_txt = text_kv[:, :, 1].astype(jnp.bfloat16)]
    unnamed x30 -> x33, local copies, waits for them, and re-layouts: 10.4 us -> 8.42 us
where the time goes in v1:
time: 329 us; the launch traced here: 327 us
  waiting for transfers between devices  183 us (56%)
  matrix products  62.6 us (19%)
  local copies, waits for them, and re-layouts  28.8 us (9%)
  other arithmetic  26.7 us (8%)
  between operations  17 us (5%)
  starting transfers between devices  9.21 us (3%)
    reduce_scatter x1, waiting for transfers between devices, local(): lax.psum_scatter(jnp.dot(mixed, w_local, preferred_element_type=jnp.float...  113 us
    all_to_all x1, waiting for transfers between devices, local(): lax.all_to_all(jnp.stack([txt_mod] * lax.axis_size('mp')), 'mp', 0, 0)  56.4 us
    sub x1, matrix products, local(): weights = jnp.exp(scores - jnp.max(scores, -1, keepdims=True))  19.6 us
    dot_general x1, matrix products, local(): jnp.einsum('hqk,khe->qhe', probs, all_values, preferred_element_type=jnp....  15 us
    all_gather x1, waiting for transfers between devices, local(): lax.all_gather(img_mod, 'mp', axis=0, tiled=True)  13.7 us
    dot_general x1, matrix products, local(): jnp.dot(img_full, w_img_qkv, preferred_element_type=jnp.float32)  11.3 us
    unnamed x33, local copies, waits for them, and re-layouts  8.42 us
    dot_general x1, matrix products, local(): jnp.dot(mixed, w_local, preferred_element_type=jnp.float32)  8.09 us
  transfers between devices with their start and end apart: 6, of which 3 were waited for; matrix products, arithmetic and copies ran while one was open for 17% of the time, Pallas kernels for 0%

profile of v1, /device:TPU:1, one launch (start us, length us, event | category | flops | bytes accessed | tf_op | source)
XLA Modules:
  0.0 327.4 jit_solution(13361720315793575944)
XLA Ops:
  7.2 1.3 dynamic_slice.51
  9.8 1.5 fusion.52
  14.4 1.9 add_convert_fusion.1
  16.3 1.3 convert_reduce_fusion
  17.6 1.5 fusion.21
  19.1 1.5 fusion.31
  20.7 2.0 stack.10
  22.7 5.8 %all-to-all-start = ((bf16[4,128,3072]{2,1,0:T(8,128)(2,1)}), bf16[4,128,3072]{2,1,0:T(8,128)(2,1)}, u32[]{:S(2)}, u32[]{:S(2)}) async-start(bf16[4,128,3072]{2,1,0:T(8,128)(2,1)} %stack.10), calls=%async_computation | async-start | bytes 6291456 | tf_op jit(solution)/shard_map/all_to_all | solution.py:71
  28.6 7.0 %copy.38 = bf16[768,3072]{1,0:T(8,128)(2,1)} copy(bf16[768,3072]{0,1:T(8,128)(2,1)} %bitcast.88) | data formatting | bytes 9437184 | tf_op jit(solution)/shard_map/dot_general | solution.py:80
  40.1 56.4 %all-to-all-done = bf16[4,128,3072]{2,1,0:T(8,128)(2,1)} async-done(((bf16[4,128,3072]{2,1,0:T(8,128)(2,1)}), bf16[4,128,3072]{2,1,0:T(8,128)(2,1)}, u32[]{:S(2)}, u32[]{:S(2)}) %all-to-all-start) | async-done | bytes 3145760 | tf_op jit(solution)/shard_map/all_to_all | solution.py:71
  96.5 6.3 %fusion.55 = f32[512,3,2,128]{3,0,2,1:T(8,128)S(1)} fusion(bf16[512,3072,1,1]{1,0,3,2:T(8,128)(2,1)} %bitcast.9, bf16[3,2,128,3072]{3,2,1,0:T(8,128)(2,1)} %bitcast.89), kind=kOutput, calls=%fused_computation.100 | convolution fusion | flops 2415919104 | bytes 9437184 | tf_op jit(solution)/shard_map/dot_general | solution.py:80
  104.2 13.7 %all-gather.2.cloned.1.call-done = bf16[1024,3072]{1,0:T(8,128)(2,1)} async-done(((bf16[256,3072]{1,0:T(8,128)(2,1)}), bf16[1024,3072]{1,0:T(8,128)(2,1)}) %all-gather.2.cloned.1.call-update) | async-done | bytes 6291472 | tf_op jit(solution)/shard_map/all_gather | solution.py:69
  117.9 11.3 %fusion.56 = f32[1024,1152]{0,1:T(8,128)S(1)} fusion(bf16[1024,3072]{1,0:T(8,128)(2,1)} %all-gather.2.cloned.1.call-done, bf16[3072,1152]{1,0:T(8,128)(2,1)} %param.21), kind=kOutput, calls=%fused_computation.101 | convolution fusion | flops 7247757312 | bytes 18087936 | tf_op jit(solution)/shard_map/dot_general | solution.py:74
  129.2 2.1 copy-done.2
  131.3 1.3 slice.61
  132.6 3.0 copy.43
  135.6 1.9 fusion.22
  137.5 1.9 fusion.24
  140.4 1.1 pad_maximum_fusion.2
  141.9 1.9 fusion.32
  143.8 1.9 copy.32
  145.8 1.5 fusion.30
  148.2 2.1 pad_maximum_fusion.1
  150.4 1.6 multiply_reduce_fusion.2
  152.6 19.6 %fusion.53 = (f32[3,1024]{1,0:T(4,128)}, f32[3,1024,3072]{2,1,0:T(8,128)}) fusion(pred[3072]{0:T(1024)(128)(4,1)S(1)} %pad_add_fusion, bf16[1536,3,128]{2,0,1:T(8,128)(2,1)} %collective-permute-done.1, bf16[1024,3,128]{2,0,1:T(8,128)(2,1)} %copy-done.4, bf16[512,3,128]{2,0,1:T(8,128)(2,1)S(1)} %multiply_convert_fusion.1, f32[1024,3,3,128]{0,3,2,1:T(8,128)} %bitcast.93, ...), kind=kOutput, calls=%fused_computation.98 | convolution fusion | flops 2461928448 | bytes 41713152 | tf_op jit(solution)/shard_map/sub | solution.py:104
  172.2 15.0 %fusion.26 = bf16[3,128,1024]{2,1,0:T(8,128)(2,1)S(1)} fusion(f32[3,1024,3072]{2,1,0:T(8,128)} %get-tuple-element.19, f32[3,1024]{1,0:T(4,128)} %get-tuple-element.18, bf16[1536,3,128]{0,2,1:T(8,128)(2,1)} %collective-permute-done, bf16[1024,3,128]{0,2,1:T(8,128)(2,1)} %copy-done.3, bf16[512,3,128]{0,2,1:T(8,128)(2,1)} %copy.32), kind=kOutput, calls=%fused_computation.43 | convolution fusion | flops 2442264576 | bytes 40906752 | tf_op jit(solution)/shard_map/hqk,khe->qhe/dot_general | solution.py:106
  187.2 8.1 %fusion.13 = f32[1024,3072]{1,0:T(8,128)} fusion(bf16[1024,384]{0,1:T(8,128)(2,1)S(1)} %bitcast.94, bf16[1536,3072]{1,0:T(8,128)(2,1)} %param.25, s32[]{:T(128)S(6)} %select_n.66), kind=kOutput, calls=%fused_computation.24 | convolution fusion | flops 2415919104 | bytes 15728644 | tf_op jit(solution)/shard_map/dot_general | solution.py:112
  195.3 1.4 dynamic-slice_add_fusion
  196.8 113.1 %reduce-scatter.2.cloned.1.call-done = f32[256,3072]{1,0:T(8,128)} async-done(((f32[1024,3072]{1,0:T(8,128)}), f32[256,3072]{1,0:T(8,128)}) %reduce-scatter.2.cloned.1.call-update) | async-done | bytes 3145744 | tf_op jit(solution)/shard_map/reduce_scatter | solution.py:111
  309.9 2.3 fusion.49
  314.0 2.8 collective-permute-start.2
  318.8 1.8 subtract_bitcast_fusion
  (67 shorter events, 14.4 us)
Async XLA Ops:
  7.2 2.6 copy-start
  7.2 110.7 %all-gather.2.cloned.1.call-start = ((), (), s32[]{:S(2)}) async-start(), calls=%async_computation.2 | async-start | bytes 7864320 | tf_op jit(solution)/shard_map/all_gather | solution.py:69
  22.7 73.8 %all-to-all-start = ((bf16[4,128,3072]{2,1,0:T(8,128)(2,1)}), bf16[4,128,3072]{2,1,0:T(8,128)(2,1)}, u32[]{:S(2)}, u32[]{:S(2)}) async-start(bf16[4,128,3072]{2,1,0:T(8,128)(2,1)} %stack.10), calls=%async_computation | async-start | bytes 6291456 | tf_op jit(solution)/shard_map/all_to_all | solution.py:71
  28.5 281.3 %reduce-scatter.2.cloned.1.call-start = ((), (), s32[]{:S(2)}) async-start(), calls=%async_computation.3 | async-start | bytes 15728640 | tf_op jit(solution)/shard_map/reduce_scatter | solution.py:111
  28.5 7.0 %copy-start.12 = (s32[2,16]{1,0:T(2,128)S(1)}, s32[2,16]{1,0:T(2,128)}, u32[]{:S(2)}) copy-start(s32[2,16]{1,0:T(2,128)} %param.34) | copy-start | bytes 388
  28.5 8.3 %copy-start.9 = (s32[16]{0:T(128)S(1)}, s32[16]{0:T(128)}, u32[]{:S(2)}) copy-start(s32[16]{0:T(128)} %param.33) | copy-start | bytes 196
  28.5 8.3 %copy-start.10 = (s32[16]{0:T(128)S(1)}, s32[16]{0:T(128)}, u32[]{:S(2)}) copy-start(s32[16]{0:T(128)} %param.32) | copy-start | bytes 196
  96.5 7.4 %copy-start.11 = (f32[128]{0:T(128)S(1)}, f32[128]{0:T(128)}, u32[]{:S(2)}) copy-start(f32[128]{0:T(128)} %param.24) | copy-start | bytes 1540
  102.8 1.1 copy-start.5
  129.2 2.1 copy-start.2
  139.4 0.9 copy-start.4
  141.4 11.1 %collective-permute-start.1 = (bf16[1536,3,128]{2,0,1:T(8,128)(2,1)}, bf16[1536,3,128]{2,0,1:T(8,128)(2,1)}, u32[]{:S(2)}, u32[]{:S(2)}) collective-permute-start(bf16[1536,3,128]{2,0,1:T(8,128)(2,1)} %pad_maximum_fusion.2), channel_id=1, source_target_pairs={{0,4},{4,0},{8,12},{12,8},{16,20},{20,16},{24,28},{28,24},{32,36},... | collective-permute-start | bytes 3538952 | tf_op jit(solution)/shard_map/ppermute | solution.py:12
  147.3 0.9 copy-start.3
  150.3 21.9 %collective-permute-start = (bf16[1536,3,128]{0,2,1:T(8,128)(2,1)}, bf16[1536,3,128]{0,2,1:T(8,128)(2,1)}, u32[]{:S(2)}, u32[]{:S(2)}) collective-permute-start(bf16[1536,3,128]{0,2,1:T(8,128)(2,1)} %pad_maximum_fusion.1), channel_id=1, source_target_pairs={{0,4},{4,0},{8,12},{12,8},{16,20},{20,16},{24,28},{28,24},{32,36},... | collective-permute-start | bytes 3538952 | tf_op jit(solution)/shard_map/ppermute | solution.py:12
  312.2 0.7 copy-start.7
  312.2 0.7 copy-start.8
  312.2 1.1 copy-start.13
  312.2 8.4 %copy-start.1 = (bf16[64,3072]{1,0:T(8,128)(2,1)S(1)}, bf16[64,3072]{1,0:T(8,128)(2,1)}, u32[]{:S(2)}) copy-start(bf16[64,3072]{1,0:T(8,128)(2,1)} %param.20) | copy-start | bytes 1179652
  312.2 5.3 %copy-start.14 = (f32[8]{0:T(128)S(1)}, f32[8]{0:T(128)}, u32[]{:S(2)}) copy-start(f32[8]{0:T(128)} %param.31) | copy-start | bytes 100
  312.3 5.9 %copy-start.15 = (f32[16]{0:T(128)S(1)}, f32[16]{0:T(128)}, u32[]{:S(2)}) copy-start(f32[16]{0:T(128)} %param.30) | copy-start | bytes 196
  312.3 6.5 %copy-start.6 = (f32[256,64]{0,1:T(8,128)S(1)}, f32[256,64]{0,1:T(8,128)}, u32[]{:S(2)}) copy-start(f32[256,64]{0,1:T(8,128)} %param.18) | copy-start | bytes 196612
  314.0 4.7 %collective-permute-start.2 = (bf16[256,64]{0,1:T(8,128)(2,1)S(1)}, bf16[256,64]{0,1:T(8,128)(2,1)S(1)}, u32[]{:S(2)}, u32[]{:S(2)}) collective-permute-start(bf16[256,64]{0,1:T(8,128)(2,1)S(1)} %get-tuple-element.20), channel_id=1, source_target_pairs={{0,64},{64,0},{1,65},{65,1},{2,66},{66,2},{3,67},{67,3},{4,68},{68... | collective-permute-start | bytes 98312 | tf_op jit(solution)/shard_map/ppermute | solution.py:12
Sparse Core Ops, SparseCore 0:
  16.4 101.4 all-gather.1
  195.4 114.3 reduce-scatter.1
